TPU v7x, 256 devices: a whole 4x4x8 slice. The times are simulated.
256 devices in a mesh: layer: 4 (over y), front: 64 (over z, x, core).
Axes of the slice: x: 4, y: 4, z: 8, core: 2. Of those that a mesh axis runs over, the one named last changes fastest.
Arguments:
- right_sides: float32 [4, 2, 4, 8192], P('layer', None, None, 'front'), may hold values from -6 to 6
- leaf_inverse: bfloat16 [4, 2, 8192, 128], P('layer', None, 'front'), may hold values from -0.375 to 0.375
- couple_above: bfloat16 [4, 2, 8192, 128], P('layer', None, 'front'), may hold values from -0.1875 to 0.1875
- couple_below: bfloat16 [4, 2, 8192, 128], P('layer', None, 'front'), may hold values from -0.1875 to 0.1875
- sep_gather: bfloat16 [4, 2, 5120, 8192], P('layer', None, None, 'front'), may hold values from -0.046875 to 0.046875
- sep_inverse: bfloat16 [4, 2, 5120, 5120], P('layer', None, 'front'), may hold values from -0.0625 to 0.0625
- sep_spread: bfloat16 [4, 2, 8192, 5120], P('layer', None, 'front'), may hold values from -0.0625 to 0.0625
- panel_owner: int32 [4, 64], P('layer'), may hold values from 0 to 63, each once within a row
Outputs:
- solution: float32 [4, 2, 4, 8192], P('layer', None, None, 'front')
Inputs may be any that keep to these rules, and one draw needn't show every extreme that they name: Each row of panel_owner names every slot 0 to 63 once.
All inputs are finite; a program needn't handle non-finite values.
Results may differ from a plain program's by a relative error of at most 0.023.
Values may be sent and summed in bfloat16 or wider, within the bound.
A program may use at most 128 MiB of HBM per device.

v0:
```python
import jax
import jax.numpy as jnp
from jax import lax
from jax.sharding import PartitionSpec as P


def from_behind(block, axis, distance):
    devices = range(lax.axis_size(axis))
    route = [(i - distance, i) for i in devices if i - distance in devices]
    return lax.ppermute(block, axis, route)


def dense_apply(matrix, vector):

    def single(left, right):
        return jnp.dot(right, left.T, preferred_element_type=jnp.float32)

    real_part = single(matrix[0], vector[0]) - single(matrix[1], vector[1])
    imag_part = single(matrix[0], vector[1]) + single(matrix[1], vector[0])
    return jnp.stack([real_part, imag_part])


def layer_solve(source, leaf, gather_map, sep_panel, spread, owner_row):
    leaf_values = dense_apply(leaf, source.astype(jnp.bfloat16))
    partial_sums = dense_apply(gather_map, leaf_values.astype(jnp.bfloat16))
    sep_rounded = lax.psum(partial_sums, "front").astype(jnp.bfloat16)
    own_rows = dense_apply(sep_panel, sep_rounded).astype(jnp.bfloat16)
    stored = lax.all_gather(own_rows, "front", axis=2, tiled=True)
    count = stored.shape[1]
    panels = stored.reshape(2, count, owner_row.shape[0], own_rows.shape[2])
    sep_values = jnp.take(panels, owner_row, axis=2).reshape(2, count, stored.shape[2])
    return leaf_values - dense_apply(spread, sep_values)


def local(
    right_sides,
    leaf_inverse,
    couple_above,
    couple_below,
    sep_gather,
    sep_inverse,
    sep_spread,
    panel_owner,
):
    depth = lax.axis_size("layer")
    owner_row = panel_owner[0]
    sources = right_sides[0]

    def solve(source):
        return layer_solve(
            source, leaf_inverse[0], sep_gather[0], sep_inverse[0], sep_spread[0], owner_row
        )

    forward = solve(sources)
    for step_index in range(depth - 1):
        from_prev = from_behind(forward.astype(jnp.bfloat16), "layer", 1)
        forward = solve(sources - dense_apply(couple_above[0], from_prev))
    solution = forward
    for step_index in range(depth - 1):
        from_next = from_behind(solution.astype(jnp.bfloat16), "layer", -1)
        solution = forward - solve(dense_apply(couple_below[0], from_next))
    return solution[None]


def solution(mesh):
    return jax.shard_map(
        local,
        mesh=mesh,
        in_specs=(
            P("layer", None, None, "front"),
            P("layer", None, "front", None),
            P("layer", None, "front", None),
            P("layer", None, "front", None),
            P("layer", None, None, "front"),
            P("layer", None, "front", None),
            P("layer", None, "front", None),
            P("layer", None),
        ),
        out_specs=P("layer", None, None, "front"),
        check_vma=False,
    )
```

profile of v0, /device:TPU:1, one launch (start us, length us, event | category | flops | bytes accessed | tf_op | source)
XLA Modules:
  0.0 2287.0 jit_solution(15067838010511855414)
XLA Ops:
  5.8 1.8 fusion.108
  7.5 1.8 fusion.110
  10.3 249.5 %all-reduce.7 = bf16[2,4,5120]{2,1,0:T(4,128)(2,1)S(1)} all-reduce(f32[2,4,5120]{2,1,0:T(4,128)S(1)} %pad_maximum_fusion), channel_id=1, replica_groups=mesh['layer'=4,'front'=64] {'front'}, use_global_device_ids=true, to_apply=%region_0.0 | all-reduce | flops 40960 | bytes 245760 | tf_op jit(solution)/shard_map/psum | solution.py:26
  259.8 1.6 fusion.280
  263.7 58.7 %all_gather.21 = bf16[2,4,5120]{1,0,2:T(2,128)(2,1)} all-gather(bf16[2,4,80]{1,0,2:T(2,128)(2,1)S(1)} %copy.58), channel_id=1, replica_groups=mesh['layer'=4,'front'=64] {'front'}, dimensions={2}, use_global_device_ids=true | all-gather | bytes 83200 | tf_op jit(solution)/shard_map/all_gather | solution.py:28
  322.4 5.4 copy.60
  329.1 1.9 fusion.40
  331.0 1.8 fusion.38
  333.7 3.2 collective-permute-start
  340.8 243.3 %all-reduce.8 = bf16[2,4,5120]{2,1,0:T(4,128)(2,1)S(1)} all-reduce(f32[2,4,5120]{2,1,0:T(4,128)S(1)} %pad_maximum_fusion.1), channel_id=1, replica_groups=mesh['layer'=4,'front'=64] {'front'}, use_global_device_ids=true, to_apply=%region_1.0 | all-reduce | flops 40960 | bytes 245760 | tf_op jit(solution)/shard_map/psum | solution.py:26
  588.0 59.3 %all_gather.22 = bf16[2,4,5120]{1,0,2:T(2,128)(2,1)} all-gather(bf16[2,4,80]{1,0,2:T(2,128)(2,1)S(1)} %copy.63), channel_id=1, replica_groups=mesh['layer'=4,'front'=64] {'front'}, dimensions={2}, use_global_device_ids=true | all-gather | bytes 83200 | tf_op jit(solution)/shard_map/all_gather | solution.py:28
  647.2 5.4 copy.65
  653.7 1.8 fusion.36
  655.7 1.9 fusion.34
  657.6 1.8 fusion.127
  659.8 3.6 collective-permute-start.1
  667.2 243.3 %all-reduce.9 = bf16[2,4,5120]{2,1,0:T(4,128)(2,1)S(1)} all-reduce(f32[2,4,5120]{2,1,0:T(4,128)S(1)} %pad_maximum_fusion.2), channel_id=1, replica_groups=mesh['layer'=4,'front'=64] {'front'}, use_global_device_ids=true, to_apply=%region_2.4 | all-reduce | flops 40960 | bytes 245760 | tf_op jit(solution)/shard_map/psum | solution.py:26
  910.5 1.6 fusion.272
  914.4 58.7 %all_gather.23 = bf16[2,4,5120]{1,0,2:T(2,128)(2,1)} all-gather(bf16[2,4,80]{1,0,2:T(2,128)(2,1)S(1)} %copy.68), channel_id=1, replica_groups=mesh['layer'=4,'front'=64] {'front'}, dimensions={2}, use_global_device_ids=true | all-gather | bytes 83200 | tf_op jit(solution)/shard_map/all_gather | solution.py:28
  973.1 5.4 copy.70
  979.6 1.8 fusion.32
  981.6 1.9 fusion.30
  983.5 1.8 fusion.139
  985.7 3.6 collective-permute-start.2
  993.1 243.5 %all-reduce.10 = bf16[2,4,5120]{2,1,0:T(4,128)(2,1)S(1)} all-reduce(f32[2,4,5120]{2,1,0:T(4,128)S(1)} %pad_maximum_fusion.3), channel_id=1, replica_groups=mesh['layer'=4,'front'=64] {'front'}, use_global_device_ids=true, to_apply=%region_3.5 | all-reduce | flops 40960 | bytes 245760 | tf_op jit(solution)/shard_map/psum | solution.py:26
  1240.5 58.7 %all_gather.24 = bf16[2,4,5120]{1,0,2:T(2,128)(2,1)} all-gather(bf16[2,4,80]{1,0,2:T(2,128)(2,1)S(1)} %copy.73), channel_id=1, replica_groups=mesh['layer'=4,'front'=64] {'front'}, dimensions={2}, use_global_device_ids=true | all-gather | bytes 83200 | tf_op jit(solution)/shard_map/all_gather | solution.py:28
  1299.2 5.4 copy.75
  1305.7 1.8 fusion.28
  1307.7 1.9 fusion.26
  1309.6 1.8 fusion.148
  1313.2 3.3 collective-permute-done.3
  1319.5 243.3 %all-reduce.11 = bf16[2,4,5120]{2,1,0:T(4,128)(2,1)S(1)} all-reduce(f32[2,4,5120]{2,1,0:T(4,128)S(1)} %pad_maximum_fusion.4), channel_id=1, replica_groups=mesh['layer'=4,'front'=64] {'front'}, use_global_device_ids=true, to_apply=%region_4.6 | all-reduce | flops 40960 | bytes 245760 | tf_op jit(solution)/shard_map/psum | solution.py:26
  1566.7 58.7 %all_gather.25 = bf16[2,4,5120]{1,0,2:T(2,128)(2,1)} all-gather(bf16[2,4,80]{1,0,2:T(2,128)(2,1)S(1)} %copy.78), channel_id=1, replica_groups=mesh['layer'=4,'front'=64] {'front'}, dimensions={2}, use_global_device_ids=true | all-gather | bytes 83200 | tf_op jit(solution)/shard_map/all_gather | solution.py:28
  1625.4 5.4 copy.80
  1631.9 1.8 fusion.24
  1633.9 1.9 fusion.22
  1635.8 1.8 fusion.157
  1639.6 2.8 collective-permute-done.4
  1645.4 243.3 %all-reduce.12 = bf16[2,4,5120]{2,1,0:T(4,128)(2,1)S(1)} all-reduce(f32[2,4,5120]{2,1,0:T(4,128)S(1)} %pad_maximum_fusion.5), channel_id=1, replica_groups=mesh['layer'=4,'front'=64] {'front'}, use_global_device_ids=true, to_apply=%region_5.7 | all-reduce | flops 40960 | bytes 245760 | tf_op jit(solution)/shard_map/psum | solution.py:26
  1892.6 58.7 %all_gather.26 = bf16[2,4,5120]{1,0,2:T(2,128)(2,1)} all-gather(bf16[2,4,80]{1,0,2:T(2,128)(2,1)S(1)} %copy.83), channel_id=1, replica_groups=mesh['layer'=4,'front'=64] {'front'}, dimensions={2}, use_global_device_ids=true | all-gather | bytes 83200 | tf_op jit(solution)/shard_map/all_gather | solution.py:28
  1951.3 5.4 copy.85
  1957.9 1.8 fusion.20
  1959.8 1.9 fusion.18
  1961.7 1.8 fusion.169
  1965.3 3.0 collective-permute-done.5
  1971.3 243.4 %all-reduce.13 = bf16[2,4,5120]{2,1,0:T(4,128)(2,1)S(1)} all-reduce(f32[2,4,5120]{2,1,0:T(4,128)S(1)} %pad_maximum_fusion.6), channel_id=1, replica_groups=mesh['layer'=4,'front'=64] {'front'}, use_global_device_ids=true, to_apply=%region_6.8 | all-reduce | flops 40960 | bytes 245760 | tf_op jit(solution)/shard_map/psum | solution.py:26
  2218.5 59.0 %all_gather.27 = bf16[2,4,5120]{1,0,2:T(2,128)(2,1)} all-gather(bf16[2,4,80]{1,0,2:T(2,128)(2,1)S(1)} %copy.88), channel_id=1, replica_groups=mesh['layer'=4,'front'=64] {'front'}, dimensions={2}, use_global_device_ids=true | all-gather | bytes 83200 | tf_op jit(solution)/shard_map/all_gather | solution.py:28
  2277.5 5.5 copy.90
  (249 shorter events, 69.6 us)
Async XLA Ops:
  0.0 9.3 copy-start
  259.8 3.1 copy-start.12
  329.1 3.7 copy-start.1
  332.8 4.9 copy-start.9
  332.8 5.4 copy-start.11
  332.8 5.5 copy-start.8
  333.7 3.9 collective-permute-start
  584.1 3.1 copy-start.13
  655.6 3.7 copy-start.2
  659.8 4.3 collective-permute-start.1
  910.5 3.1 copy-start.14
  981.6 3.7 copy-start.3
  985.7 4.3 collective-permute-start.2
  1236.6 3.1 copy-start.15
  1307.7 3.7 copy-start.4
  1309.6 6.9 copy-start.10
  1311.9 4.6 collective-permute-start.3
  1562.8 3.1 copy-start.16
  1633.9 3.7 copy-start.5
  1638.0 4.3 collective-permute-start.4
  1888.7 3.1 copy-start.17
  1959.8 3.7 copy-start.6
  1964.0 4.3 collective-permute-start.5
  1971.3 246.4 %copy-start.18 = (bf16[1,2,80,5120]{3,2,1,0:T(8,128)(2,1)S(1)}, bf16[1,2,80,5120]{3,2,1,0:T(8,128)(2,1)}, u32[]{:S(2)}) copy-start(bf16[1,2,80,5120]{3,2,1,0:T(8,128)(2,1)} %param.15) | copy-start | bytes 4915204
  2277.5 6.7 copy-start.7
where the time goes:
time: 2300 us; the launch traced here: 2290 us
  blocking collectives  2120 us (92%)
  matrix products  87.5 us (4%)
  local copies, waits for them, and re-layouts  46.7 us (2%)
    psum x7, blocking collectives, layer_solve(): sep_rounded = lax.psum(partial_sums, 'front').astype(jnp.bfloat16)  1710 us
    all_gather x7, blocking collectives, layer_solve(): stored = lax.all_gather(own_rows, 'front', axis=2, tiled=True)  412 us
    dot_general x136, matrix products, single(): return jnp.dot(right, left.T, preferred_element_type=jnp.float32)  87.5 us
  transfers between devices with their start and end apart: 6, of which 6 were waited for; matrix products, arithmetic and copies ran while one was open for 0% of the time, Pallas kernels for 0%

commit v1 on v0

--- a/solution.py
+++ b/solution.py
@@ -23,7 +23,7 @@
 def layer_solve(source, leaf, gather_map, sep_panel, spread, owner_row):
     leaf_values = dense_apply(leaf, source.astype(jnp.bfloat16))
     partial_sums = dense_apply(gather_map, leaf_values.astype(jnp.bfloat16))
-    sep_rounded = lax.psum(partial_sums, "front").astype(jnp.bfloat16)
+    sep_rounded = jnp.sum(lax.all_gather(partial_sums, "front"), axis=0).astype(jnp.bfloat16)
     own_rows = dense_apply(sep_panel, sep_rounded).astype(jnp.bfloat16)
     stored = lax.all_gather(own_rows, "front", axis=2, tiled=True)
     count = stored.shape[1]

time: 2300 us -> 1210 us (0.53)
  blocking collectives: 2120 us -> 384 us
  waiting for transfers between devices: 11.3 us -> 611 us
  other arithmetic: 4.45 us -> 50.4 us
    psum x7 -> x0, blocking collectives: 1710 us -> none  [layer_solve(): sep_rounded = lax.psum(partial_sums, 'front').astype(jnp.bfloat16)]
    all_gather x0 -> x7, waiting for transfers between devices: none -> 599 us  [layer_solve(): lax.all_gather(partial_sums, 'front')]
    reduce_sum x0 -> x7, other arithmetic: none -> 42.5 us  [layer_solve(): jnp.sum(lax.all_gather(partial_sums, 'front'), axis=0).astype(jnp.bfloat16)]
    all_gather x7, blocking collectives: 412 us -> 384 us  [layer_solve(): stored = lax.all_gather(own_rows, 'front', axis=2, tiled=True)]
  transfers between devices with their start and end apart: 6 -> 13, of which waited for: 6 -> 13; matrix products, arithmetic and copies ran while one was open for 0% -> 0% of each run, Pallas kernels for 0% -> 0%
where the time goes in v1:
time: 1210 us
  waiting for transfers between devices  611 us (50%)
  blocking collectives  384 us (32%)
  matrix products  85.3 us (7%)
  other arithmetic  50.4 us (4%)
  local copies, waits for them, and re-layouts  46.7 us (4%)
  between operations  14.7 us (1%)
  starting transfers between devices  13.7 us (1%)
    all_gather x7, waiting for transfers between devices, layer_solve(): lax.all_gather(partial_sums, 'front')  599 us
    all_gather x7, blocking collectives, layer_solve(): stored = lax.all_gather(own_rows, 'front', axis=2, tiled=True)  384 us
    dot_general x136, matrix products, single(): return jnp.dot(right, left.T, preferred_element_type=jnp.float32)  85.3 us
    reduce_sum x7, other arithmetic, layer_solve(): jnp.sum(lax.all_gather(partial_sums, 'front'), axis=0).astype(jnp.bfloat16)  42.5 us
    reshape x7, local copies, waits for them, and re-layouts, layer_solve(): panels = stored.reshape(2, count, owner_row.shape[0], own_rows.shape[2])  37.8 us
  transfers between devices with their start and end apart: 13, of which 13 were waited for; matrix products, arithmetic and copies ran while one was open for 0% of the time, Pallas kernels for 0%

profile of v1, /device:TPU:1, one launch (start us, length us, event | category | flops | bytes accessed | tf_op | source)
XLA Modules:
  0.0 1205.4 jit_solution(17404388164355153193)
XLA Ops:
  11.0 1.8 fusion.108
  12.8 1.8 fusion.110
  16.3 90.6 %all-gather.15.cloned.1.call-done = f32[128,4,5120]{2,1,0:T(4,128)} async-done(((f32[2,4,5120]{2,1,0:T(4,128)}), f32[128,4,5120]{2,1,0:T(4,128)}) %all-gather.15.cloned.1.call-update) | async-done | bytes 10485776 | tf_op jit(solution)/shard_map/all_gather | solution.py:26
  106.9 6.1 reduce_sum.63
  116.9 54.7 %all_gather.65 = bf16[2,4,5120]{1,0,2:T(2,128)(2,1)} all-gather(bf16[2,4,80]{1,0,2:T(2,128)(2,1)S(1)} %copy.58), channel_id=1, replica_groups=mesh['layer'=4,'front'=64] {'front'}, dimensions={2}, use_global_device_ids=true | all-gather | bytes 83200 | tf_op jit(solution)/shard_map/all_gather | solution.py:28
  171.5 5.4 copy.60
  178.2 1.9 fusion.40
  180.1 1.8 fusion.38
  182.8 3.1 collective-permute-start
  190.7 84.8 %all-gather.17.cloned.1.call-done = f32[128,4,5120]{2,1,0:T(4,128)} async-done(((f32[2,4,5120]{2,1,0:T(4,128)}), f32[128,4,5120]{2,1,0:T(4,128)}) %all-gather.17.cloned.1.call-update) | async-done | bytes 10485776 | tf_op jit(solution)/shard_map/all_gather | solution.py:26
  275.6 6.1 reduce_sum.64
  285.5 54.7 %all_gather.68 = bf16[2,4,5120]{1,0,2:T(2,128)(2,1)} all-gather(bf16[2,4,80]{1,0,2:T(2,128)(2,1)S(1)} %copy.63), channel_id=1, replica_groups=mesh['layer'=4,'front'=64] {'front'}, dimensions={2}, use_global_device_ids=true | all-gather | bytes 83200 | tf_op jit(solution)/shard_map/all_gather | solution.py:28
  340.2 5.4 copy.65
  348.6 1.9 fusion.34
  350.5 1.8 fusion.127
  352.8 3.1 collective-permute-start.1
  360.4 85.0 %all-gather.19.cloned.1.call-done = f32[128,4,5120]{2,1,0:T(4,128)} async-done(((f32[2,4,5120]{2,1,0:T(4,128)}), f32[128,4,5120]{2,1,0:T(4,128)}) %all-gather.19.cloned.1.call-update) | async-done | bytes 10485776 | tf_op jit(solution)/shard_map/all_gather | solution.py:26
  445.5 6.1 reduce_sum.65
  455.4 55.1 %all_gather.71 = bf16[2,4,5120]{1,0,2:T(2,128)(2,1)} all-gather(bf16[2,4,80]{1,0,2:T(2,128)(2,1)S(1)} %copy.68), channel_id=1, replica_groups=mesh['layer'=4,'front'=64] {'front'}, dimensions={2}, use_global_device_ids=true | all-gather | bytes 83200 | tf_op jit(solution)/shard_map/all_gather | solution.py:28
  510.5 5.4 copy.70
  519.0 1.9 fusion.30
  520.9 1.8 fusion.139
  523.1 3.1 collective-permute-start.2
  530.8 85.0 %all-gather.21.cloned.1.call-done = f32[128,4,5120]{2,1,0:T(4,128)} async-done(((f32[2,4,5120]{2,1,0:T(4,128)}), f32[128,4,5120]{2,1,0:T(4,128)}) %all-gather.21.cloned.1.call-update) | async-done | bytes 10485776 | tf_op jit(solution)/shard_map/all_gather | solution.py:26
  615.8 6.1 reduce_sum.66
  625.7 54.8 %all_gather.74 = bf16[2,4,5120]{1,0,2:T(2,128)(2,1)} all-gather(bf16[2,4,80]{1,0,2:T(2,128)(2,1)S(1)} %copy.73), channel_id=1, replica_groups=mesh['layer'=4,'front'=64] {'front'}, dimensions={2}, use_global_device_ids=true | all-gather | bytes 83200 | tf_op jit(solution)/shard_map/all_gather | solution.py:28
  680.6 5.4 copy.75
  689.0 1.9 fusion.26
  690.9 1.8 fusion.148
  694.5 3.0 collective-permute-done.3
  701.4 84.6 %all-gather.23.cloned.1.call-done = f32[128,4,5120]{2,1,0:T(4,128)} async-done(((f32[2,4,5120]{2,1,0:T(4,128)}), f32[128,4,5120]{2,1,0:T(4,128)}) %all-gather.23.cloned.1.call-update) | async-done | bytes 10485776 | tf_op jit(solution)/shard_map/all_gather | solution.py:26
  785.9 6.1 reduce_sum.67
  795.9 54.9 %all_gather.77 = bf16[2,4,5120]{1,0,2:T(2,128)(2,1)} all-gather(bf16[2,4,80]{1,0,2:T(2,128)(2,1)S(1)} %copy.78), channel_id=1, replica_groups=mesh['layer'=4,'front'=64] {'front'}, dimensions={2}, use_global_device_ids=true | all-gather | bytes 83200 | tf_op jit(solution)/shard_map/all_gather | solution.py:28
  850.7 5.4 copy.80
  859.2 1.9 fusion.22
  861.1 1.8 fusion.157
  864.7 3.0 collective-permute-done.4
  871.5 84.6 %all-gather.25.cloned.1.call-done = f32[128,4,5120]{2,1,0:T(4,128)} async-done(((f32[2,4,5120]{2,1,0:T(4,128)}), f32[128,4,5120]{2,1,0:T(4,128)}) %all-gather.25.cloned.1.call-update) | async-done | bytes 10485776 | tf_op jit(solution)/shard_map/all_gather | solution.py:26
  956.1 6.1 reduce_sum.68
  966.0 54.9 %all_gather.80 = bf16[2,4,5120]{1,0,2:T(2,128)(2,1)} all-gather(bf16[2,4,80]{1,0,2:T(2,128)(2,1)S(1)} %copy.83), channel_id=1, replica_groups=mesh['layer'=4,'front'=64] {'front'}, dimensions={2}, use_global_device_ids=true | all-gather | bytes 83200 | tf_op jit(solution)/shard_map/all_gather | solution.py:28
  1020.9 5.4 copy.85
  1029.4 1.9 fusion.18
  1031.3 1.8 fusion.169
  1034.8 3.0 collective-permute-done.5
  1041.6 84.6 %all-gather.27.cloned.1.call-done = f32[128,4,5120]{2,1,0:T(4,128)} async-done(((f32[2,4,5120]{2,1,0:T(4,128)}), f32[128,4,5120]{2,1,0:T(4,128)}) %all-gather.27.cloned.1.call-update) | async-done | bytes 10485776 | tf_op jit(solution)/shard_map/all_gather | solution.py:26
  1126.2 6.2 reduce_sum.69
  1133.9 55.0 %all_gather.83 = bf16[2,4,5120]{1,0,2:T(2,128)(2,1)} all-gather(bf16[2,4,80]{1,0,2:T(2,128)(2,1)S(1)} %copy.88), channel_id=1, replica_groups=mesh['layer'=4,'front'=64] {'front'}, dimensions={2}, use_global_device_ids=true | all-gather | bytes 83200 | tf_op jit(solution)/shard_map/all_gather | solution.py:28
  1188.8 5.5 copy.90
  (272 shorter events, 83.1 us)
Async XLA Ops:
  6.5 8.0 copy-start
  6.5 100.4 %all-gather.15.cloned.1.call-start = ((), (), s32[]{:S(2)}) async-start(), calls=%async_computation | async-start | bytes 10649600 | tf_op jit(solution)/shard_map/all_gather | solution.py:26
  14.5 1.7 copy-start.19
  16.2 259.4 %all-gather.17.cloned.1.call-start = ((), (), s32[]{:S(2)}) async-start(), calls=%async_computation.1 | async-start | bytes 10649600 | tf_op jit(solution)/shard_map/all_gather | solution.py:26
  113.0 3.1 copy-start.12
  178.2 3.7 copy-start.1
  181.9 4.8 copy-start.9
  181.9 5.3 copy-start.11
  181.9 5.4 copy-start.8
  182.8 3.8 collective-permute-start
  190.5 255.0 %all-gather.19.cloned.1.call-start = ((), (), s32[]{:S(2)}) async-start(), calls=%async_computation.2 | async-start | bytes 10649600 | tf_op jit(solution)/shard_map/all_gather | solution.py:26
  281.6 3.1 copy-start.13
  348.6 3.7 copy-start.2
  352.8 3.8 collective-permute-start.1
  360.4 255.4 %all-gather.21.cloned.1.call-start = ((), (), s32[]{:S(2)}) async-start(), calls=%async_computation.3 | async-start | bytes 10649600 | tf_op jit(solution)/shard_map/all_gather | solution.py:26
  451.5 3.1 copy-start.14
  518.9 3.7 copy-start.3
  523.1 3.8 collective-permute-start.2
  530.7 255.2 %all-gather.23.cloned.1.call-start = ((), (), s32[]{:S(2)}) async-start(), calls=%async_computation.4 | async-start | bytes 10649600 | tf_op jit(solution)/shard_map/all_gather | solution.py:26
  621.9 3.1 copy-start.15
  689.0 3.7 copy-start.4
  690.9 6.6 copy-start.10
  693.2 4.3 collective-permute-start.3
  701.3 254.7 %all-gather.25.cloned.1.call-start = ((), (), s32[]{:S(2)}) async-start(), calls=%async_computation.5 | async-start | bytes 10649600 | tf_op jit(solution)/shard_map/all_gather | solution.py:26
  792.0 3.1 copy-start.16
  859.2 3.7 copy-start.5
  863.4 4.3 collective-permute-start.4
  871.5 254.8 %all-gather.27.cloned.1.call-start = ((), (), s32[]{:S(2)}) async-start(), calls=%async_computation.6 | async-start | bytes 10649600 | tf_op jit(solution)/shard_map/all_gather | solution.py:26
  962.1 3.1 copy-start.17
  1029.4 3.7 copy-start.6
  1033.5 4.3 collective-permute-start.5
  1126.2 6.2 copy-start.18
  1188.8 6.7 copy-start.7
Sparse Core Ops, SparseCore 0:
  16.3 90.5 all-gather.14
  190.6 84.9 all-gather.16
  360.5 84.9 all-gather.18
  530.8 84.9 all-gather.20
  701.4 84.4 all-gather.22
  871.6 84.4 all-gather.24
  1041.7 84.4 all-gather.26
